TPU v7x, 32 devices: a whole 2x2x4 slice. The times are simulated.
32 devices in a mesh: dp: 16 (over z, y, core), mp: 2 (over x).
Axes of the slice: x: 2, y: 2, z: 4, core: 2. Of those that a mesh axis runs over, the one named last changes fastest.
Arguments:
- patch_counts: int32 [128], P('dp'), may hold values from 100 to 240, as said below
- tokens: bfloat16 [128, 280, 768], P('dp'), may hold values from -6 to 6
- cotangent: bfloat16 [128, 280, 768], P('dp'), may hold values from -6 to 6
- attn_gain: float32 [768], P('dp'), may hold values from 0.1 to 1.9
- attn_shift: float32 [768], P('dp'), may hold values from -1.75 to 1.75
- w_qkv: float32 [768, 3, 768], P('dp', None, 'mp'), may hold values from -0.21875 to 0.21875
- b_qv: float32 [2, 768], P(None, 'mp'), may hold values from -3 to 3
- w_proj: float32 [768, 768], P('mp', 'dp'), may hold values from -0.875 to 0.875
- b_proj: float32 [768], P('dp'), may hold values from -3 to 3
- ffn_gain: float32 [768], P('dp'), may hold values from 0.1 to 1.9
- ffn_shift: float32 [768], P('dp'), may hold values from -1.75 to 1.75
- w_up: float32 [768, 3072], P('dp', 'mp'), may hold values from -0.21875 to 0.21875
- b_up: float32 [3072], P('mp'), may hold values from -3 to 3
- w_down: float32 [3072, 768], P('mp', 'dp'), may hold values from -0.109375 to 0.109375
- b_down: float32 [768], P('dp'), may hold values from -3 to 3
Outputs:
- block_out: bfloat16 [128, 280, 768], P('dp')
- tokens_grad: bfloat16 [128, 280, 768], P('dp')
- attn_gain_grad: float32 [768], P('dp')
- attn_shift_grad: float32 [768], P('dp')
- w_qkv_grad: float32 [768, 3, 768], P('dp', None, 'mp')
- b_qv_grad: float32 [2, 768], P(None, 'mp')
- w_proj_grad: float32 [768, 768], P('mp', 'dp')
- b_proj_grad: float32 [768], P('dp')
- ffn_gain_grad: float32 [768], P('dp')
- ffn_shift_grad: float32 [768], P('dp')
- w_up_grad: float32 [768, 3072], P('dp', 'mp')
- b_up_grad: float32 [3072], P('mp')
- w_down_grad: float32 [3072, 768], P('mp', 'dp')
- b_down_grad: float32 [768], P('dp')
Inputs may be any that keep to these rules, and one draw needn't show every extreme that they name: `patch_counts`: patch count of each pair; in every draw some pair has exactly 240 patches and some exactly 100.
All inputs are finite; a program needn't handle non-finite values.
Results may differ from a plain program's by a relative error of at most 0.022.
Values may be sent and summed in bfloat16 or wider, within the bound.
A program may use at most 192 MiB of HBM per device.

v0:
```python
import math
import jax
import jax.numpy as jnp
from jax import lax
from jax.sharding import PartitionSpec as P

HEADS = 12
HEAD_DIM = 64
TEXT = 40


def normalize(values, gain, shift):
    center = values - jnp.mean(values, axis=-1, keepdims=True)
    spread = jnp.mean(center * center, axis=-1, keepdims=True)
    return center * lax.rsqrt(spread + 1e-06) * gain + shift


def norm_back(values, gain, incoming):
    _, pullback = jax.vjp(lambda member, scaling: normalize(member, scaling, 0.0), values, gain)
    d_values, d_gain = pullback(incoming)
    return (d_values, d_gain, jnp.sum(incoming, axis=(0, 1)))


def per_device(
    patch_counts,
    tokens,
    cotangent,
    attn_gain,
    attn_shift,
    w_qkv,
    b_qv,
    w_proj,
    b_proj,
    ffn_gain,
    ffn_shift,
    w_up,
    b_up,
    w_down,
    b_down,
):
    low_type = jnp.bfloat16
    pair_count, rows_pair, _ = tokens.shape
    head_count = HEADS // lax.axis_size("mp")
    local_width = w_qkv.shape[2]
    score_scale = HEAD_DIM ** (-0.5)
    pair_block = math.gcd(pair_count, -(-512 // rows_pair))
    block_count = pair_count // pair_block
    gathered = (
        lax.all_gather(w_qkv.astype(low_type), "dp", axis=0, tiled=True),
        lax.all_gather(w_proj.astype(low_type), "dp", axis=1, tiled=True),
        lax.all_gather(w_up.astype(low_type), "dp", axis=0, tiled=True),
        lax.all_gather(w_down.astype(low_type), "dp", axis=1, tiled=True),
        lax.all_gather(attn_gain.astype(low_type), "dp", axis=0, tiled=True),
        lax.all_gather(attn_shift.astype(low_type), "dp", axis=0, tiled=True),
        lax.all_gather(b_proj.astype(low_type), "dp", axis=0, tiled=True),
        lax.all_gather(ffn_gain.astype(low_type), "dp", axis=0, tiled=True),
        lax.all_gather(ffn_shift.astype(low_type), "dp", axis=0, tiled=True),
        lax.all_gather(b_down.astype(low_type), "dp", axis=0, tiled=True),
    )
    qkv_full, proj_full, up_full, down_full = (gathered[0], gathered[1], gathered[2], gathered[3])
    gain_one = gathered[4].astype(jnp.float32)
    shift_one = gathered[5].astype(jnp.float32)
    proj_bias = gathered[6].astype(jnp.float32)
    gain_two = gathered[7].astype(jnp.float32)
    shift_two = gathered[8].astype(jnp.float32)
    down_bias = gathered[9].astype(jnp.float32)
    bias_qv = b_qv.astype(low_type).astype(jnp.float32)
    up_bias = b_up.astype(low_type).astype(jnp.float32)
    row_valid = (
        jnp.arange(rows_pair, dtype=jnp.int32)[None, :] < (TEXT + patch_counts)[:, None]
    ).astype(jnp.float32)
    inputs = tokens.astype(jnp.float32)
    normed_one = normalize(inputs, gain_one, shift_one).astype(low_type)
    qkv = jnp.einsum("psd,dtc->pstc", normed_one, qkv_full, preferred_element_type=jnp.float32)
    queries = (qkv[:, :, 0] + bias_qv[0]).astype(low_type)
    key_rows = qkv[:, :, 1].astype(low_type)
    values = (qkv[:, :, 2] + bias_qv[1]).astype(low_type)

    def by_blocks(array):
        return array.reshape(block_count, pair_block, rows_pair, head_count, HEAD_DIM)

    key_mask = row_valid.reshape(block_count, pair_block, rows_pair)

    def score_rows(query_block, key_block, mask_block):
        raw = (
            jnp.einsum(
                "bqhe,bkhe->bhqk", query_block, key_block, preferred_element_type=jnp.float32
            )
            * score_scale
        )
        return jnp.where(mask_block[:, None, None, :] > 0, raw, -1e30)

    def attend(operands):
        query_block, key_block, value_block, mask_block = operands
        scores = score_rows(query_block, key_block, mask_block)
        row_max = jnp.max(scores, axis=-1, keepdims=True)
        expo = jnp.exp(scores - row_max)
        row_total = jnp.sum(expo, axis=-1, keepdims=True)
        probabilities = (expo / row_total).astype(low_type)
        attended_block = jnp.einsum(
            "bhqk,bkhe->bqhe", probabilities, value_block, preferred_element_type=jnp.float32
        ).astype(low_type)
        log_total = row_max[..., 0] + jnp.log(row_total[..., 0])
        return (attended_block, log_total)

    attended_blocks, log_totals = lax.map(
        attend, (by_blocks(queries), by_blocks(key_rows), by_blocks(values), key_mask)
    )
    attended = attended_blocks.reshape(pair_count, rows_pair, local_width)
    proj_part = jnp.einsum("psc,cd->psd", attended, proj_full, preferred_element_type=jnp.float32)
    attn_sum = lax.psum(proj_part.astype(jnp.bfloat16), "mp").astype(jnp.float32)
    hidden = inputs + attn_sum + proj_bias
    normed_two = normalize(hidden, gain_two, shift_two).astype(low_type)
    pre_act = (
        jnp.einsum("psd,df->psf", normed_two, up_full, preferred_element_type=jnp.float32) + up_bias
    )
    active = jax.nn.gelu(pre_act, approximate=False).astype(low_type)
    down_part = jnp.einsum("psf,fd->psd", active, down_full, preferred_element_type=jnp.float32)
    mlp_sum = lax.psum(down_part.astype(jnp.bfloat16), "mp").astype(jnp.float32)
    block_out = ((hidden + mlp_sum + down_bias) * row_valid[:, :, None]).astype(low_type)
    qkv_back, proj_back, up_back, down_back = (qkv_full, proj_full, up_full, down_full)
    gain_one_back, gain_two_back = (gain_one, gain_two)
    upstream = cotangent.astype(jnp.float32) * row_valid[:, :, None]
    upstream_low = upstream.astype(low_type)
    grad_b_down = jnp.sum(upstream, axis=(0, 1))
    grad_w_down = jnp.einsum(
        "psf,psd->fd", active, upstream_low, preferred_element_type=jnp.float32
    )
    d_active = jnp.einsum(
        "psd,fd->psf", upstream_low, down_back, preferred_element_type=jnp.float32
    )
    _, gelu_pull = jax.vjp(lambda member: jax.nn.gelu(member, approximate=False), pre_act)
    d_pre = gelu_pull(d_active)[0].astype(low_type)
    grad_b_up = jnp.sum(d_pre, axis=(0, 1), dtype=jnp.float32)
    grad_w_up = jnp.einsum("psd,psf->df", normed_two, d_pre, preferred_element_type=jnp.float32)
    d_normed_two = lax.psum(
        jnp.einsum("psf,df->psd", d_pre, up_back, preferred_element_type=jnp.float32).astype(
            jnp.bfloat16
        ),
        "mp",
    ).astype(jnp.float32)
    d_hidden_norm, grad_gain_two, grad_shift_two = norm_back(hidden, gain_two_back, d_normed_two)
    d_hidden = upstream + d_hidden_norm
    grad_b_proj = jnp.sum(d_hidden, axis=(0, 1))
    d_hidden_low = d_hidden.astype(low_type)
    grad_w_proj = jnp.einsum(
        "psc,psd->cd", attended, d_hidden_low, preferred_element_type=jnp.float32
    )
    d_attended = jnp.einsum(
        "psd,cd->psc", d_hidden_low, proj_back, preferred_element_type=jnp.float32
    ).astype(low_type)

    def attend_back(operands):
        query_block, key_block, value_block, mask_block, log_total, d_out = operands
        scores = score_rows(query_block, key_block, mask_block)
        probabilities = jnp.exp(scores - log_total[..., None])
        d_probs = jnp.einsum(
            "bqhe,bkhe->bhqk", d_out, value_block, preferred_element_type=jnp.float32
        )
        d_value = jnp.einsum(
            "bhqk,bqhe->bkhe",
            probabilities.astype(low_type),
            d_out,
            preferred_element_type=jnp.float32,
        )
        inner = jnp.sum(probabilities * d_probs, axis=-1, keepdims=True)
        d_scores = (probabilities * (d_probs - inner)).astype(low_type)
        d_query = score_scale * jnp.einsum(
            "bhqk,bkhe->bqhe", d_scores, key_block, preferred_element_type=jnp.float32
        )
        d_key = score_scale * jnp.einsum(
            "bhqk,bqhe->bkhe", d_scores, query_block, preferred_element_type=jnp.float32
        )
        return jnp.stack([d_query, d_key, d_value], axis=2).astype(low_type)

    d_blocks = lax.map(
        attend_back,
        (
            by_blocks(queries),
            by_blocks(key_rows),
            by_blocks(values),
            key_mask,
            log_totals,
            by_blocks(d_attended),
        ),
    )
    d_qkv = d_blocks.reshape(pair_count, rows_pair, 3, local_width)
    column_sums = jnp.sum(d_qkv, axis=(0, 1), dtype=jnp.float32)
    grad_b_qv = jnp.stack([column_sums[0], column_sums[2]], axis=0)
    grad_w_qkv = jnp.einsum("psd,pstc->dtc", normed_one, d_qkv, preferred_element_type=jnp.float32)
    d_normed_one = lax.psum(
        jnp.einsum("pstc,dtc->psd", d_qkv, qkv_back, preferred_element_type=jnp.float32).astype(
            jnp.bfloat16
        ),
        "mp",
    ).astype(jnp.float32)
    d_input_norm, grad_gain_one, grad_shift_one = norm_back(inputs, gain_one_back, d_normed_one)
    tokens_grad = (d_hidden + d_input_norm).astype(low_type)
    bias_grads = lax.psum((grad_b_qv, grad_b_up), "dp")
    summed = (
        lax.psum_scatter(grad_w_qkv, "dp", scatter_dimension=0, tiled=True),
        lax.psum_scatter(grad_w_proj, "dp", scatter_dimension=1, tiled=True),
        lax.psum_scatter(grad_w_up, "dp", scatter_dimension=0, tiled=True),
        lax.psum_scatter(grad_w_down, "dp", scatter_dimension=1, tiled=True),
        lax.psum_scatter(grad_gain_one, "dp", scatter_dimension=0, tiled=True),
        lax.psum_scatter(grad_shift_one, "dp", scatter_dimension=0, tiled=True),
        lax.psum_scatter(grad_b_proj, "dp", scatter_dimension=0, tiled=True),
        lax.psum_scatter(grad_gain_two, "dp", scatter_dimension=0, tiled=True),
        lax.psum_scatter(grad_shift_two, "dp", scatter_dimension=0, tiled=True),
        lax.psum_scatter(grad_b_down, "dp", scatter_dimension=0, tiled=True),
    )
    out_qkv, out_proj, out_up, out_down = (summed[0], summed[1], summed[2], summed[3])
    out_gain_one, out_shift_one, out_bproj = (summed[4], summed[5], summed[6])
    out_gain_two, out_shift_two, out_bdown = (summed[7], summed[8], summed[9])
    return (
        block_out,
        tokens_grad,
        out_gain_one,
        out_shift_one,
        out_qkv,
        bias_grads[0],
        out_proj,
        out_bproj,
        out_gain_two,
        out_shift_two,
        out_up,
        bias_grads[1],
        out_down,
        out_bdown,
    )


def solution(mesh):
    in_specs = (
        P("dp"),
        P("dp", None, None),
        P("dp", None, None),
        P("dp"),
        P("dp"),
        P("dp", None, "mp"),
        P(None, "mp"),
        P("mp", "dp"),
        P("dp"),
        P("dp"),
        P("dp"),
        P("dp", "mp"),
        P("mp"),
        P("mp", "dp"),
        P("dp"),
    )
    out_specs = (
        P("dp", None, None),
        P("dp", None, None),
        P("dp"),
        P("dp"),
        P("dp", None, "mp"),
        P(None, "mp"),
        P("mp", "dp"),
        P("dp"),
        P("dp"),
        P("dp"),
        P("dp", "mp"),
        P("mp"),
        P("mp", "dp"),
        P("dp"),
    )
    return jax.shard_map(
        per_device, mesh=mesh, in_specs=in_specs, out_specs=out_specs, check_vma=False
    )
```

profile of v0, /device:TPU:0, one launch (start us, length us, event | category | flops | bytes accessed | tf_op | source)
XLA Modules:
  0.0 1070.2 jit_solution(13060933296893398383)
XLA Ops:
  20.8 63.2 %all-reduce.13 = (bf16[768]{0:T(1024)(128)(2,1)}, bf16[768]{0:T(1024)(128)(2,1)}, bf16[768]{0:T(1024)(128)(2,1)}, bf16[768]{0:T(1024)(128)(2,1)}, bf16[768]{0:T(1024)(128)(2,1)}, /*index=5*/bf16[768]{0:T(1024)(128)(2,1)}) all-reduce(bf16[768]{0:T(1024)(128)(2,1)} %dynamic-update-slice.4, ...), channel_id=1, replica_groups=mesh['dp'=16,'mp'=2] {'dp'}, use_global_device_ids=true, to_apply=%add.4 | all-reduce | flops 4608 | bytes 18432
  97.2 20.3 %all_gather.33 = bf16[384,768]{0,1:T(8,128)(2,1)} all-gather(bf16[384,48]{0,1:T(8,128)(2,1)S(1)} %convert_element_type.183), channel_id=1, replica_groups=mesh['dp'=16,'mp'=2] {'dp'}, dimensions={1}, use_global_device_ids=true | all-gather | bytes 626688 | tf_op jit(solution)/shard_map/all_gather | solution.py:50
  117.5 7.1 fusion.96
  124.6 3.3 fusion.113
  129.4 6.0 copy.58
  135.3 5.5 copy.59
  140.8 4.0 copy.60
  144.8 7.3 add_convert_fusion.3
  152.2 32.6 %while.22 = (s32[]{:T(128)}, bf16[4,2,280,6,64]{2,4,3,1,0:T(8,128)(2,1)}, f32[4,2,6,280]{3,2,1,0:T(8,128)S(1)}, bf16[4,2,280,6,64]{2,4,3,1,0:T(8,128)(2,1)}, f32...) while((s32[]{:T(128)}, ...), condition=%wide.region_5.6_spmd, body=%wide.region_2.5_spmd.sunk | while | flops 252346640 | bytes 13796445 | solution.py:106
  156.9 3.5 fusion.145
  165.0 3.5 fusion.145
  173.2 3.5 fusion.145
  181.3 3.5 fusion.145
  184.8 6.0 convolution_convert_fusion.2
  198.1 83.8 %all-reduce.19.cloned.1.call-done = bf16[8,280,768]{2,1,0:T(8,128)(2,1)} async-done(((bf16[8,280,768]{2,1,0:T(8,128)(2,1)}), bf16[8,280,768]{2,1,0:T(8,128)(2,1)}) %all-reduce.19.cloned.1.call-update) | async-done | bytes 3440656 | tf_op jit(solution)/shard_map/psum | solution.py:111
  281.9 3.3 fusion.82
  288.5 38.6 %all-gather.6.cloned.1.call-done = bf16[768,1536]{1,0:T(8,128)(2,1)} async-done(((bf16[48,1536]{1,0:T(8,128)(2,1)}), bf16[768,1536]{1,0:T(8,128)(2,1)}) %all-gather.6.cloned.1.call-update) | async-done | bytes 2359312 | tf_op jit(solution)/shard_map/all_gather | solution.py:51
  327.1 13.9 %fusion.86 = (u8[280,1536]{1,0:T(8,128)(4,1)S(1)}, u8[280,1536]{1,0:T(8,128)(4,1)S(1)}, f32[8,280,1536]{2,1,0:T(8,128)S(1)}) fusion(f32[1536]{0:T(1024)} %convert_convert_fusion, bf16[768,1536]{1,0:T(8,128)(2,1)} %all-gather.6.cloned.1.call-done, f32[768]{0:T(1024)} %convert_element_type.191, f32[768]{0:T(1024)} %convert_element_type.189, ...), kind=kOutput, calls=%fused_computation.134 | convolution fusion | flops 5347614720 | bytes 23896576 | tf_op jit(solution)/shard_map/psd,df->psf/dot_general | solution.py:115
  341.0 4.9 copy-done.6
  346.0 32.9 %multiply_convert_fusion.1 = (bf16[8,280,1536]{2,1,0:T(8,128)(2,1)}, f32[8,280,1536]{2,1,0:T(8,128)}) fusion(f32[8,280,1536]{2,1,0:T(8,128)S(1)} %get-tuple-element.187, f32[1536]{0:T(1024)S(1)} %copy-done.25, u8[280,1536]{1,0:T(8,128)(4,1)S(1)} %get-tuple-element.113, u8[280,1536]{1,0:T(8,128)(4,1)S(1)} %get-tuple-element.112), kind=kLoop, calls=%fused_computation.75 | loop fusion | flops 244285440 | bytes 35272704 | tf_op jit(solution)/shard_map/convert_element_type | solution.py:117
  378.9 18.8 %convert_reduce_fusion.1 = (f32[1536]{0:T(1024)}, bf16[8,280,1536]{2,1,0:T(8,128)(2,1)}) fusion(f32[8,280,1536]{2,1,0:T(8,128)} %get-tuple-element.173, bf16[1536,768]{0,1:T(8,128)(2,1)} %all-gather.8.cloned.1.call-done, bf16[8,280,768]{2,1,0:T(8,128)(2,1)} %param.21, f32[8,280]{1,0:T(8,128)} %fusion.108, f32[8,280,1536]{2,1,0:T(8,128)} %copy-done.6, ...), kind=kOutput, calls=%fused_computation.73 | convolution fusion | flops 5348473344 | bytes 40227584 | tf_op jit(solution)/shard_map/psd,fd->psf/dot_general | solution.py:129
  397.6 10.0 convolution_convert_fusion
  407.7 10.0 convolution_convert_fusion.1
  417.7 81.1 %all-reduce.21.cloned.1.call-done = bf16[8,280,768]{2,1,0:T(8,128)(2,1)} async-done(((bf16[8,280,768]{2,1,0:T(8,128)(2,1)}), bf16[8,280,768]{2,1,0:T(8,128)(2,1)}) %all-reduce.21.cloned.1.call-update) | async-done | bytes 3440656 | tf_op jit(solution)/shard_map/psum | solution.py:136
  498.8 6.4 convert_reduce_fusion.3
  505.2 5.6 fusion.77
  510.8 4.9 fusion.111
  521.6 4.0 copy.62
  525.6 64.1 %while.23 = (s32[]{:T(128)}, bf16[4,2,280,3,6,64]{2,5,4,1,3,0:T(8,128)(2,1)}, bf16[4,2,280,6,64]{2,4,3,1,0:T(8,128)(2,1)}, f32[4,2,280]{2,1,0:T(2,128)}, bf16[4,...) while((s32[]{:T(128)}, ...), condition=%wide.region_15.16_spmd, body=%wide.region_13.15_spmd.sunk | while | flops 621167104 | bytes 36805476 | solution.py:176
  529.1 3.4 multiply_reduce_fusion.3
  545.0 3.4 multiply_reduce_fusion.3
  560.9 3.4 multiply_reduce_fusion.3
  576.8 3.4 multiply_reduce_fusion.3
  589.7 4.3 copy.63
  596.9 7.7 bitcast_convert_fusion
  604.8 7.4 fusion.101
  612.3 12.6 %convolution_bitcast_fusion.1 = f32[768,1536]{1,0:T(8,128)} fusion(bf16[8,280,1536]{2,1,0:T(8,128)(2,1)} %get-tuple-element.189, f32[768]{0:T(1024)S(1)} %copy-done.35, f32[768]{0:T(1024)S(1)} %copy-done.24, f32[8,280]{1,0:T(8,128)S(1)} %copy-done.20, f32[8,280]{1,0:T(8,128)S(1)} %broadcast_multiply_fusion, f32[768]{0:T(1024)S(1)} %convert_element_type.187, ...), kind=kOutput, calls=%fused_computation.130 | convolution fusion | flops 5300305920 | bytes 18508288 | tf_op jit(solution)/shard_map/psd,psf->df/dot_general | solution.py:135
  625.0 11.0 %convolution_bitcast_fusion = f32[1536,768]{0,1:T(8,128)} fusion(bf16[8,280,1536]{2,1,0:T(8,128)(2,1)} %get-tuple-element.172, bf16[8,280,768]{2,1,0:T(8,128)(2,1)} %param.21, f32[8,280]{1,0:T(8,128)S(1)} %copy-done.18), kind=kOutput, calls=%fused_computation.129 | convolution fusion | flops 5289984000 | bytes 15049472 | tf_op jit(solution)/shard_map/psf,psd->fd/dot_general | solution.py:126
  636.3 13.7 %convolution_bitcast_fusion.2 = f32[768,3,384]{2,0,1:T(8,128)} fusion(bf16[8,280,3,384]{1,3,2,0:T(8,128)(2,1)} %bitcast.170, bf16[8,280,768]{2,1,0:T(8,128)(2,1)S(1)} %copy-done, f32[768]{0:T(1024)S(1)} %copy-done.34, f32[768]{0:T(1024)S(1)} %copy-done.22, f32[8,280]{1,0:T(8,128)S(1)} %copy-done.16, f32[8,280]{1,0:T(8,128)S(1)} %copy-done.11), kind=kOutput, calls=%fused_computation.144 | convolution fusion | flops 3973939200 | bytes 12164608 | tf_op jit(solution)/shard_map/psd,pstc->dtc/dot_general | solution.py:190
  650.7 4.3 convert_reduce_fusion
  655.3 115.5 %all-reduce.23.cloned.1.call-done = (bf16[8,280,768]{2,1,0:T(8,128)(2,1)}, bf16[8,280,768]{2,1,0:T(8,128)(2,1)}) async-done(((bf16[8,280,768]{2,1,0:T(8,128)(2,1)}, bf16[8,280,768]{2,1,0:T(8,128)(2,1)}), (bf16[8,280,768]{2,1,0:T(8,128)(2,1)}, bf16[8,280,768]{2,1,0:T(8,128)(2,1)})) %all-reduce.23.cloned.1.call-update) | async-done | bytes 6881296 | tf_op jit(solution)/shard_map/psum | solution.py:119
  770.7 4.2 convert_reduce_fusion.2
  774.9 4.3 fusion.78
  779.3 61.8 %all-reduce.12 = (f32[768]{0:T(1024)S(1)}, f32[768]{0:T(1024)S(1)}, f32[2,384]{1,0:T(2,128)}, f32[768]{0:T(1024)}, f32[768]{0:T(1024)}, /*index=5*/f32[768]{0:T(1024)}, f32[1536]{0:T(1024)}, f32[768]{0:T(1024)S(1)}) all-reduce(f32[768]{0:T(1024)S(1)} %get-tuple-element.116, ...), channel_id=2, replica_groups=mesh['dp'=16,'mp'=2] {'dp'}, use_global_device_ids=true, to_apply=%region_20.21.clone | all-reduce | flops 6912 | bytes 55296
  846.6 11.0 %add_convert_fusion.1 = (bf16[8,280,768]{2,1,0:T(8,128)(2,1)}, bf16[8,280,768]{2,1,0:T(8,128)(2,1)}) fusion(f32[8,280,768]{2,1,0:T(8,128)} %copy-done.3, bf16[8,280,768]{2,1,0:T(8,128)(2,1)S(1)} %copy-done, bf16[8,280,768]{2,1,0:T(8,128)(2,1)} %get-tuple-element.169, f32[8,280]{1,0:T(8,128)S(1)} %negate_multiply_fusion.1, ...), kind=kLoop, calls=%fused_computation.116 | loop fusion | flops 32686080 | bytes 27579136 | tf_op jit(solution)/shard_map/convert_element_type | solution.py:198
  857.6 54.7 %reduce-scatter.9.cloned.1.call-done = f32[48,1536]{1,0:T(8,128)} async-done(((f32[768,1536]{1,0:T(8,128)}), f32[48,1536]{1,0:T(8,128)}) %reduce-scatter.9.cloned.1.call-update) | async-done | bytes 294928 | tf_op jit(solution)/shard_map/reduce_scatter | solution.py:203
  912.3 79.2 %reduce-scatter.11.cloned.1.call-done = f32[1536,48]{0,1:T(8,128)} async-done(((f32[1536,768]{0,1:T(8,128)}), f32[1536,48]{0,1:T(8,128)}) %reduce-scatter.11.cloned.1.call-update) | async-done | bytes 294928 | tf_op jit(solution)/shard_map/reduce_scatter | solution.py:204
  991.5 71.6 %reduce-scatter.5.cloned.1.call-done = f32[48,3,384]{2,0,1:T(8,128)} async-done(((f32[768,3,384]{2,0,1:T(8,128)}), f32[48,3,384]{2,0,1:T(8,128)}) %reduce-scatter.5.cloned.1.call-update) | async-done | bytes 221200 | tf_op jit(solution)/shard_map/reduce_scatter | solution.py:201
  (218 shorter events, 122.1 us)
Async XLA Ops:
  7.2 110.4 %copy-start = (bf16[8,280,768]{2,1,0:T(8,128)(2,1)S(1)}, bf16[8,280,768]{2,1,0:T(8,128)(2,1)}, u32[]{:S(2)}) copy-start(bf16[8,280,768]{2,1,0:T(8,128)(2,1)} %param.20) | copy-start | bytes 10321924
  7.2 110.3 %all-gather.4.cloned.1.call-start = ((), (), s32[]{:S(2)}) async-start(), calls=%async_computation.4 | async-start | bytes 1880064 | tf_op jit(solution)/shard_map/all_gather | solution.py:49
  9.0 272.9 %all-reduce.19.cloned.1.call-start = ((), (), s32[]{:S(2)}) async-start(), calls=%async_computation.5 | async-start | bytes 6881280 | tf_op jit(solution)/shard_map/psum | solution.py:111
  84.7 39.9 %copy-start.21 = (f32[768]{0:T(1024)}, f32[768]{0:T(1024)S(1)}, u32[]{:S(2)}) copy-start(f32[768]{0:T(1024)S(1)} %convert_element_type.172) | copy-start | bytes 9220
  92.9 31.7 %copy-start.10 = (f32[8,280]{1,0:T(8,128)}, f32[8,280]{1,0:T(8,128)S(1)}, u32[]{:S(2)}) copy-start(f32[8,280]{1,0:T(8,128)S(1)} %broadcast_multiply_fusion.1) | copy-start | bytes 26884
  135.3 9.5 copy-start.28
  135.3 9.5 copy-start.29
  184.8 9.5 copy-start.39
  184.8 12.1 %copy-start.37 = (bf16[768]{0:T(1024)(128)(2,1)S(1)}, bf16[768]{0:T(1024)(128)(2,1)}, u32[]{:S(2)}) copy-start(bf16[768]{0:T(1024)(128)(2,1)} %get-tuple-element.162) | copy-start | bytes 4612
  184.8 12.7 %copy-start.32 = (f32[1536]{0:T(1024)S(1)}, f32[1536]{0:T(1024)}, u32[]{:S(2)}) copy-start(f32[1536]{0:T(1024)} %param.31) | copy-start | bytes 18436
  190.8 136.3 %all-gather.6.cloned.1.call-start = ((), (), s32[]{:S(2)}) async-start(), calls=%async_computation.6 | async-start | bytes 2506752 | tf_op jit(solution)/shard_map/all_gather | solution.py:51
  192.5 186.3 %all-gather.8.cloned.1.call-start = ((), (), s32[]{:S(2)}) async-start(), calls=%async_computation.7 | async-start | bytes 2506752 | tf_op jit(solution)/shard_map/all_gather | solution.py:52
  194.2 304.6 %all-reduce.21.cloned.1.call-start = ((), (), s32[]{:S(2)}) async-start(), calls=%async_computation.8 | async-start | bytes 6881280 | tf_op jit(solution)/shard_map/psum | solution.py:136
  281.9 3.3 copy-start.1
  327.1 18.9 %copy-start.25 = (f32[1536]{0:T(1024)S(1)}, f32[1536]{0:T(1024)}, u32[]{:S(2)}) copy-start(f32[1536]{0:T(1024)} %convert_convert_fusion) | copy-start | bytes 18436
  341.0 5.0 copy-start.6
  378.9 18.8 %copy-start.40 = (bf16[768,1536]{1,0:T(8,128)(2,1)S(1)}, bf16[768,1536]{1,0:T(8,128)(2,1)}, u32[]{:S(2)}) copy-start(bf16[768,1536]{1,0:T(8,128)(2,1)} %all-gather.6.cloned.1.call-done) | copy-start | bytes 7077892
  407.7 363.0 %all-reduce.23.cloned.1.call-start = ((), (), s32[]{:S(2)}) async-start(), calls=%async_computation.13 | async-start | bytes 13762560 | tf_op jit(solution)/shard_map/psum | solution.py:119
  498.8 6.4 copy-start.15
  498.8 6.4 copy-start.2
  498.8 6.4 copy-start.5
  498.8 6.4 copy-start.19
  498.8 6.4 copy-start.23
  505.2 5.6 copy-start.8
  505.2 5.6 copy-start.17
  510.8 7.6 copy-start.9
  515.7 2.8 copy-start.3
  589.7 7.2 copy-start.41
  594.0 2.9 copy-start.7
  604.6 7.7 copy-start.20
  604.6 7.7 copy-start.24
  604.6 7.7 copy-start.35
  604.6 253.0 %reduce-scatter.7.cloned.1.call-start = ((), (), s32[]{:S(2)}) async-start(), calls=%async_computation.10 | async-start | bytes 1253376 | tf_op jit(solution)/shard_map/reduce_scatter | solution.py:202
  612.2 12.8 %copy-start.18 = (f32[8,280]{1,0:T(8,128)S(1)}, f32[8,280]{1,0:T(8,128)}, u32[]{:S(2)}) copy-start(f32[8,280]{1,0:T(8,128)} %fusion.108) | copy-start | bytes 26884
  612.2 300.1 %reduce-scatter.9.cloned.1.call-start = ((), (), s32[]{:S(2)}) async-start(), calls=%async_computation.11 | async-start | bytes 5013504 | tf_op jit(solution)/shard_map/reduce_scatter | solution.py:203
  624.9 11.4 %copy-start.11 = (f32[8,280]{1,0:T(8,128)S(1)}, f32[8,280]{1,0:T(8,128)}, u32[]{:S(2)}) copy-start(f32[8,280]{1,0:T(8,128)} %copy-done.10) | copy-start | bytes 26884
  624.9 11.4 %copy-start.16 = (f32[8,280]{1,0:T(8,128)S(1)}, f32[8,280]{1,0:T(8,128)}, u32[]{:S(2)}) copy-start(f32[8,280]{1,0:T(8,128)} %fusion.109) | copy-start | bytes 26884
  624.9 11.4 %copy-start.22 = (f32[768]{0:T(1024)S(1)}, f32[768]{0:T(1024)}, u32[]{:S(2)}) copy-start(f32[768]{0:T(1024)} %copy-done.21) | copy-start | bytes 9220
  624.9 11.4 %copy-start.34 = (f32[768]{0:T(1024)S(1)}, f32[768]{0:T(1024)}, u32[]{:S(2)}) copy-start(f32[768]{0:T(1024)} %convert_element_type.174) | copy-start | bytes 9220
  624.9 366.6 %reduce-scatter.11.cloned.1.call-start = ((), (), s32[]{:S(2)}) async-start(), calls=%async_computation.12 | async-start | bytes 5013504 | tf_op jit(solution)/shard_map/reduce_scatter | solution.py:204
  636.0 14.1 %copy-start.36 = (bf16[768]{0:T(1024)(128)(2,1)S(1)}, bf16[768]{0:T(1024)(128)(2,1)}, u32[]{:S(2)}) copy-start(bf16[768]{0:T(1024)(128)(2,1)} %get-tuple-element.167) | copy-start | bytes 4612
  636.0 427.1 %reduce-scatter.5.cloned.1.call-start = ((), (), s32[]{:S(2)}) async-start(), calls=%async_computation.9 | async-start | bytes 3760128 | tf_op jit(solution)/shard_map/reduce_scatter | solution.py:201
  650.7 124.2 %copy-start.13 = (f32[8,280]{1,0:T(8,128)S(1)}, f32[8,280]{1,0:T(8,128)}, u32[]{:S(2)}) copy-start(f32[8,280]{1,0:T(8,128)} %copy-done.12) | copy-start | bytes 26884
  770.7 4.2 copy-start.4
  770.7 8.5 copy-start.26
  770.7 8.5 copy-start.27
  770.7 8.5 copy-start.30
  770.7 8.5 copy-start.31
  (4 other events, 3.4 us)
Sparse Core Ops, SparseCore 0:
  10.9 43.1 all-gather.3
  190.9 90.9 all-reduce.18
  284.8 42.3 all-gather.5
  329.8 41.0 all-gather.7
  407.8 90.9 all-reduce.20
  604.7 165.9 all-reduce.22
  774.9 58.1 reduce-scatter.6
  837.6 74.6 reduce-scatter.8
  916.7 74.7 reduce-scatter.10
  995.8 67.3 reduce-scatter.4
where the time goes:
time: 1080 us; the launch traced here: 1070 us
  waiting for transfers between devices  525 us (49%)
  matrix products  194 us (18%)
  blocking collectives  145 us (13%)
  other arithmetic  136 us (13%)
  local copies, waits for them, and re-layouts  53.1 us (5%)
  between operations  16.2 us (2%)
    unnamed x2, blocking collectives  125 us
    psum x1, waiting for transfers between devices, per_device(): mlp_sum = lax.psum(down_part.astype(jnp.bfloat16), 'mp').astype(jnp.float32)  115 us
    psum x1, waiting for transfers between devices, per_device(): lax.psum(proj_part.astype(jnp.bfloat16), 'mp').astype(jnp.float32)  83.8 us
    psum x1, waiting for transfers between devices, per_device(): lax.psum(jnp.einsum('psf,df->psd', d_pre, up_back, preferred_element_type...  81.1 us
    reduce_scatter x1, waiting for transfers between devices, per_device(): lax.psum_scatter(grad_w_down, 'dp', scatter_dimension=1, tiled=True)  79.2 us
    reduce_scatter x1, waiting for transfers between devices, per_device(): lax.psum_scatter(grad_w_qkv, 'dp', scatter_dimension=0, tiled=True)  71.6 us
    reduce_scatter x1, waiting for transfers between devices, per_device(): lax.psum_scatter(grad_w_up, 'dp', scatter_dimension=0, tiled=True)  54.7 us
    all_gather x1, waiting for transfers between devices, per_device(): lax.all_gather(w_up.astype(low_type), 'dp', axis=0, tiled=True)  38.6 us
  transfers between devices with their start and end apart: 10, of which 7 were waited for; matrix products, arithmetic and copies ran while one was open for 16% of the time, Pallas kernels for 0%

commit v1 on v0

--- a/solution.py
+++ b/solution.py
@@ -7,6 +7,18 @@
 HEADS = 12
 HEAD_DIM = 64
 TEXT = 40
+
+
+def doubled_up(array, axis, dim):
+    ways, here = (lax.axis_size(axis), lax.axis_index(axis))
+    grown, reach = (array, 1)
+    while reach < ways:
+        theirs = lax.ppermute(grown, axis, [(d, d ^ reach) for d in range(ways)])
+        mine_first = jnp.concatenate([grown, theirs], axis=dim)
+        theirs_first = jnp.concatenate([theirs, grown], axis=dim)
+        grown = jnp.where(here & reach == 0, mine_first, theirs_first)
+        reach = 2 * reach
+    return grown
 
 
 def normalize(values, gain, shift):
@@ -48,7 +60,7 @@
     gathered = (
         lax.all_gather(w_qkv.astype(low_type), "dp", axis=0, tiled=True),
         lax.all_gather(w_proj.astype(low_type), "dp", axis=1, tiled=True),
-        lax.all_gather(w_up.astype(low_type), "dp", axis=0, tiled=True),
+        doubled_up(w_up.astype(low_type), "dp", 0),
         lax.all_gather(w_down.astype(low_type), "dp", axis=1, tiled=True),
         lax.all_gather(attn_gain.astype(low_type), "dp", axis=0, tiled=True),
         lax.all_gather(attn_shift.astype(low_type), "dp", axis=0, tiled=True),

time: 1080 us -> 1040 us (0.963)
  waiting for transfers between devices: 525 us -> 477 us
    all_gather x1 -> x0, waiting for transfers between devices: 38.6 us -> none  [per_device(): lax.all_gather(w_up.astype(low_type), 'dp', axis=0, tiled=True)]
    psum x1, waiting for transfers between devices: 83.8 us -> 55.2 us  [per_device(): lax.psum(proj_part.astype(jnp.bfloat16), 'mp').astype(jnp.float32)]
    ppermute x0 -> x4, waiting for transfers between devices: none -> 18.3 us  [doubled_up(): theirs = lax.ppermute(grown, axis, [(d, d ^ reach) for d in range(ways)])]
    unnamed x103 -> x99, local copies, waits for them, and re-layouts: 23.1 us -> 18.1 us
  transfers between devices with their start and end apart: 10 -> 13, of which waited for: 7 -> 9; matrix products, arithmetic and copies ran while one was open for 16% -> 18% of each run, Pallas kernels for 0% -> 0%
where the time goes in v1:
time: 1040 us; the launch traced here: 1030 us
  waiting for transfers between devices  477 us (46%)
  matrix products  199 us (19%)
  other arithmetic  145 us (14%)
  blocking collectives  145 us (14%)
  local copies, waits for them, and re-layouts  47.8 us (5%)
  between operations  15.9 us (2%)
    unnamed x2, blocking collectives  125 us
    psum x1, waiting for transfers between devices, per_device(): mlp_sum = lax.psum(down_part.astype(jnp.bfloat16), 'mp').astype(jnp.float32)  115 us
    psum x1, waiting for transfers between devices, per_device(): lax.psum(jnp.einsum('psf,df->psd', d_pre, up_back, preferred_element_type...  82.5 us
    reduce_scatter x1, waiting for transfers between devices, per_device(): lax.psum_scatter(grad_w_down, 'dp', scatter_dimension=1, tiled=True)  79.2 us
    reduce_scatter x1, waiting for transfers between devices, per_device(): lax.psum_scatter(grad_w_qkv, 'dp', scatter_dimension=0, tiled=True)  71.9 us
    psum x1, waiting for transfers between devices, per_device(): lax.psum(proj_part.astype(jnp.bfloat16), 'mp').astype(jnp.float32)  55.2 us
    reduce_scatter x1, waiting for transfers between devices, per_device(): lax.psum_scatter(grad_w_up, 'dp', scatter_dimension=0, tiled=True)  54.5 us
    convert_element_type x1, other arithmetic, per_device(): active = jax.nn.gelu(pre_act, approximate=False).astype(low_type)  34.4 us
  transfers between devices with their start and end apart: 13, of which 9 were waited for; matrix products, arithmetic and copies ran while one was open for 18% of the time, Pallas kernels for 0%

profile of v1, /device:TPU:0, one launch (start us, length us, event | category | flops | bytes accessed | tf_op | source)
XLA Modules:
  0.0 1033.5 jit_solution(330288182911182065)
XLA Ops:
  20.8 63.2 %all-reduce.13 = (bf16[768]{0:T(1024)(128)(2,1)}, bf16[768]{0:T(1024)(128)(2,1)}, bf16[768]{0:T(1024)(128)(2,1)}, bf16[768]{0:T(1024)(128)(2,1)}, bf16[768]{0:T(1024)(128)(2,1)}, /*index=5*/bf16[768]{0:T(1024)(128)(2,1)}) all-reduce(bf16[768]{0:T(1024)(128)(2,1)} %dynamic-update-slice.4, ...), channel_id=1, replica_groups=mesh['dp'=16,'mp'=2] {'dp'}, use_global_device_ids=true, to_apply=%add.4 | all-reduce | flops 4608 | bytes 18432
  97.2 20.3 %all_gather.30 = bf16[384,768]{0,1:T(8,128)(2,1)} all-gather(bf16[384,48]{0,1:T(8,128)(2,1)S(1)} %convert_element_type.183), channel_id=1, replica_groups=mesh['dp'=16,'mp'=2] {'dp'}, dimensions={1}, use_global_device_ids=true | all-gather | bytes 626688 | tf_op jit(solution)/shard_map/all_gather | solution.py:62
  117.5 7.1 fusion.94
  124.6 3.3 fusion.116
  129.3 5.7 copy.58
  135.0 5.5 copy.59
  140.5 4.0 copy.60
  144.5 7.3 add_convert_fusion.3
  151.8 32.6 %while.22 = (s32[]{:T(128)}, bf16[4,2,280,6,64]{2,4,3,1,0:T(8,128)(2,1)}, f32[4,2,6,280]{3,2,1,0:T(8,128)S(1)}, bf16[4,2,280,6,64]{2,4,3,1,0:T(8,128)(2,1)}, f32...) while((s32[]{:T(128)}, ...), condition=%wide.region_5.6_spmd, body=%wide.region_2.5_spmd.sunk | while | flops 252346640 | bytes 13796445 | solution.py:118
  156.5 3.5 fusion.148
  164.7 3.5 fusion.148
  172.9 3.5 fusion.148
  181.0 3.5 fusion.148
  184.5 6.0 convolution_convert_fusion.2
  198.0 7.8 collective-permute-done.1
  214.3 9.1 collective-permute-done.2
  226.4 55.2 %all-reduce.19.cloned.1.call-done = bf16[8,280,768]{2,1,0:T(8,128)(2,1)} async-done(((bf16[8,280,768]{2,1,0:T(8,128)(2,1)}), bf16[8,280,768]{2,1,0:T(8,128)(2,1)}) %all-reduce.19.cloned.1.call-update) | async-done | bytes 3440656 | tf_op jit(solution)/shard_map/psum | solution.py:123
  281.6 3.3 fusion.82
  287.6 18.2 %fusion.86 = (u8[280,1536]{1,0:T(8,128)(4,1)S(1)}, u8[280,1536]{1,0:T(8,128)(4,1)S(1)}, f32[8,280,1536]{2,1,0:T(8,128)}) fusion(f32[1536]{0:T(1024)} %convert_convert_fusion, bf16[384,1536]{1,0:T(8,128)(2,1)} %collective-permute-done.3, bf16[384,1536]{1,0:T(8,128)(2,1)} %maximum_select_fusion.1, pred[]{:T(512)S(6)} %eq.12, f32[768]{0:T(1024)} %convert_element_type.191, ...), kind=kOutput, calls=%fused_computation.134 | convolution fusion | flops 5358231552 | bytes 23896576 | tf_op jit(solution)/shard_map/psd,df->psf/dot_general | solution.py:127
  305.9 34.4 %multiply_convert_fusion.1 = (bf16[8,280,1536]{2,1,0:T(8,128)(2,1)}, f32[8,280,1536]{2,1,0:T(8,128)}) fusion(f32[8,280,1536]{2,1,0:T(8,128)} %get-tuple-element.187, f32[1536]{0:T(1024)S(1)} %copy-done.25, u8[280,1536]{1,0:T(8,128)(4,1)S(1)} %get-tuple-element.113, u8[280,1536]{1,0:T(8,128)(4,1)S(1)} %get-tuple-element.112), kind=kLoop, calls=%fused_computation.75 | loop fusion | flops 244285440 | bytes 35272704 | tf_op jit(solution)/shard_map/convert_element_type | solution.py:129
  340.3 18.5 %convert_reduce_fusion.1 = (f32[1536]{0:T(1024)}, bf16[8,280,1536]{2,1,0:T(8,128)(2,1)}) fusion(f32[8,280,1536]{2,1,0:T(8,128)} %get-tuple-element.173, bf16[1536,768]{0,1:T(8,128)(2,1)} %all-gather.5.cloned.1.call-done, bf16[8,280,768]{2,1,0:T(8,128)(2,1)} %param.21, f32[8,280]{1,0:T(8,128)} %fusion.109, f32[8,280,1536]{2,1,0:T(8,128)} %get-tuple-element.187, ...), kind=kOutput, calls=%fused_computation.73 | convolution fusion | flops 5348473344 | bytes 40227584 | tf_op jit(solution)/shard_map/psd,fd->psf/dot_general | solution.py:141
  358.8 11.4 %convolution_convert_fusion = bf16[8,280,768]{2,1,0:T(8,128)(2,1)} fusion(bf16[8,280,1536]{2,1,0:T(8,128)(2,1)} %get-tuple-element.189, bf16[384,1536]{1,0:T(8,128)(2,1)} %collective-permute-done.3, bf16[384,1536]{1,0:T(8,128)(2,1)} %maximum_select_fusion.1, pred[]{:T(512)S(6)} %eq.12), kind=kOutput, calls=%fused_computation.136 | convolution fusion | flops 5297160192 | bytes 12681217 | tf_op jit(solution)/shard_map/psf,df->psd/dot_general | solution.py:149
  370.3 9.9 convolution_convert_fusion.1
  380.2 82.5 %all-reduce.21.cloned.1.call-done = bf16[8,280,768]{2,1,0:T(8,128)(2,1)} async-done(((bf16[8,280,768]{2,1,0:T(8,128)(2,1)}), bf16[8,280,768]{2,1,0:T(8,128)(2,1)}) %all-reduce.21.cloned.1.call-update) | async-done | bytes 3440656 | tf_op jit(solution)/shard_map/psum | solution.py:148
  462.7 6.4 convert_reduce_fusion.3
  469.1 5.6 fusion.77
  474.7 4.9 fusion.114
  485.5 4.0 copy.62
  489.4 63.9 %while.23 = (s32[]{:T(128)}, bf16[4,2,280,3,6,64]{2,5,4,1,3,0:T(8,128)(2,1)}, bf16[4,2,280,6,64]{2,4,3,1,0:T(8,128)(2,1)}, f32[4,2,280]{2,1,0:T(2,128)}, bf16[4,...) while((s32[]{:T(128)}, ...), condition=%wide.region_15.16_spmd, body=%wide.region_13.15_spmd.sunk | while | flops 621167104 | bytes 36805476 | solution.py:188
  492.7 3.4 multiply_reduce_fusion.3
  508.6 3.4 multiply_reduce_fusion.3
  524.5 3.4 multiply_reduce_fusion.3
  540.4 3.4 multiply_reduce_fusion.3
  553.3 4.3 copy.63
  560.5 7.7 bitcast_convert_fusion
  568.6 7.4 fusion.102
  576.1 12.6 %convolution_bitcast_fusion.1 = f32[768,1536]{1,0:T(8,128)} fusion(bf16[8,280,1536]{2,1,0:T(8,128)(2,1)} %get-tuple-element.189, f32[768]{0:T(1024)S(1)} %copy-done.35, f32[768]{0:T(1024)S(1)} %copy-done.24, f32[8,280]{1,0:T(8,128)S(1)} %copy-done.20, f32[8,280]{1,0:T(8,128)S(1)} %broadcast_multiply_fusion, f32[768]{0:T(1024)S(1)} %convert_element_type.187, ...), kind=kOutput, calls=%fused_computation.130 | convolution fusion | flops 5300305920 | bytes 18508288 | tf_op jit(solution)/shard_map/psd,psf->df/dot_general | solution.py:147
  588.8 11.0 %convolution_bitcast_fusion = f32[1536,768]{0,1:T(8,128)} fusion(bf16[8,280,1536]{2,1,0:T(8,128)(2,1)} %get-tuple-element.172, bf16[8,280,768]{2,1,0:T(8,128)(2,1)} %param.21, f32[8,280]{1,0:T(8,128)S(1)} %copy-done.17), kind=kOutput, calls=%fused_computation.129 | convolution fusion | flops 5289984000 | bytes 15049472 | tf_op jit(solution)/shard_map/psf,psd->fd/dot_general | solution.py:138
  600.1 13.7 %convolution_bitcast_fusion.2 = f32[768,3,384]{2,0,1:T(8,128)} fusion(bf16[8,280,3,384]{1,3,2,0:T(8,128)(2,1)} %bitcast.169, bf16[8,280,768]{2,1,0:T(8,128)(2,1)S(1)} %copy-done, f32[768]{0:T(1024)S(1)} %copy-done.34, f32[768]{0:T(1024)S(1)} %copy-done.22, f32[8,280]{1,0:T(8,128)S(1)} %copy-done.15, f32[8,280]{1,0:T(8,128)S(1)} %copy-done.10), kind=kOutput, calls=%fused_computation.143 | convolution fusion | flops 3973939200 | bytes 12164608 | tf_op jit(solution)/shard_map/psd,pstc->dtc/dot_general | solution.py:202
  614.5 4.3 convert_reduce_fusion
  619.0 115.3 %all-reduce.23.cloned.1.call-done = (bf16[8,280,768]{2,1,0:T(8,128)(2,1)}, bf16[8,280,768]{2,1,0:T(8,128)(2,1)}) async-done(((bf16[8,280,768]{2,1,0:T(8,128)(2,1)}, bf16[8,280,768]{2,1,0:T(8,128)(2,1)}), (bf16[8,280,768]{2,1,0:T(8,128)(2,1)}, bf16[8,280,768]{2,1,0:T(8,128)(2,1)})) %all-reduce.23.cloned.1.call-update) | async-done | bytes 6881296 | tf_op jit(solution)/shard_map/psum | solution.py:131
  734.3 4.2 convert_reduce_fusion.2
  738.5 4.3 fusion.78
  742.9 61.8 %all-reduce.12 = (f32[768]{0:T(1024)S(1)}, f32[768]{0:T(1024)S(1)}, f32[2,384]{1,0:T(2,128)}, f32[768]{0:T(1024)}, f32[768]{0:T(1024)}, /*index=5*/f32[768]{0:T(1024)}, f32[1536]{0:T(1024)}, f32[768]{0:T(1024)S(1)}) all-reduce(f32[768]{0:T(1024)S(1)} %get-tuple-element.116, ...), channel_id=2, replica_groups=mesh['dp'=16,'mp'=2] {'dp'}, use_global_device_ids=true, to_apply=%region_20.21.clone | all-reduce | flops 6912 | bytes 55296
  810.2 11.0 %add_convert_fusion.1 = (bf16[8,280,768]{2,1,0:T(8,128)(2,1)}, bf16[8,280,768]{2,1,0:T(8,128)(2,1)}) fusion(f32[8,280,768]{2,1,0:T(8,128)} %copy-done.3, bf16[8,280,768]{2,1,0:T(8,128)(2,1)S(1)} %copy-done, bf16[8,280,768]{2,1,0:T(8,128)(2,1)} %get-tuple-element.169, f32[8,280]{1,0:T(8,128)S(1)} %negate_multiply_fusion.1, ...), kind=kLoop, calls=%fused_computation.116 | loop fusion | flops 32686080 | bytes 27579136 | tf_op jit(solution)/shard_map/convert_element_type | solution.py:210
  821.2 54.5 %reduce-scatter.9.cloned.1.call-done = f32[48,1536]{1,0:T(8,128)} async-done(((f32[768,1536]{1,0:T(8,128)}), f32[48,1536]{1,0:T(8,128)}) %reduce-scatter.9.cloned.1.call-update) | async-done | bytes 294928 | tf_op jit(solution)/shard_map/reduce_scatter | solution.py:215
  875.7 79.2 %reduce-scatter.11.cloned.1.call-done = f32[1536,48]{0,1:T(8,128)} async-done(((f32[1536,768]{0,1:T(8,128)}), f32[1536,48]{0,1:T(8,128)}) %reduce-scatter.11.cloned.1.call-update) | async-done | bytes 294928 | tf_op jit(solution)/shard_map/reduce_scatter | solution.py:216
  954.9 71.9 %reduce-scatter.5.cloned.1.call-done = f32[48,3,384]{2,0,1:T(8,128)} async-done(((f32[768,3,384]{2,0,1:T(8,128)}), f32[48,3,384]{2,0,1:T(8,128)}) %reduce-scatter.5.cloned.1.call-update) | async-done | bytes 221200 | tf_op jit(solution)/shard_map/reduce_scatter | solution.py:213
  (222 shorter events, 133.4 us)
Async XLA Ops:
  7.2 110.3 %copy-start = (bf16[8,280,768]{2,1,0:T(8,128)(2,1)S(1)}, bf16[8,280,768]{2,1,0:T(8,128)(2,1)}, u32[]{:S(2)}) copy-start(bf16[8,280,768]{2,1,0:T(8,128)(2,1)} %param.20) | copy-start | bytes 10321924
  7.2 110.3 %all-gather.3.cloned.1.call-start = ((), (), s32[]{:S(2)}) async-start(), calls=%async_computation.4 | async-start | bytes 1880064 | tf_op jit(solution)/shard_map/all_gather | solution.py:61
  9.0 272.5 %all-reduce.19.cloned.1.call-start = ((), (), s32[]{:S(2)}) async-start(), calls=%async_computation.5 | async-start | bytes 6881280 | tf_op jit(solution)/shard_map/psum | solution.py:123
  84.7 39.9 %copy-start.21 = (f32[768]{0:T(1024)}, f32[768]{0:T(1024)S(1)}, u32[]{:S(2)}) copy-start(f32[768]{0:T(1024)S(1)} %convert_element_type.172) | copy-start | bytes 9220
  92.9 31.7 %copy-start.9 = (f32[8,280]{1,0:T(8,128)}, f32[8,280]{1,0:T(8,128)S(1)}, u32[]{:S(2)}) copy-start(f32[8,280]{1,0:T(8,128)S(1)} %broadcast_multiply_fusion.1) | copy-start | bytes 26884
  135.0 9.5 copy-start.28
  135.0 9.5 copy-start.29
  184.5 27.4 %copy-start.37 = (bf16[768]{0:T(1024)(128)(2,1)S(1)}, bf16[768]{0:T(1024)(128)(2,1)}, u32[]{:S(2)}) copy-start(bf16[768]{0:T(1024)(128)(2,1)} %get-tuple-element.162) | copy-start | bytes 4612
  184.5 29.3 %copy-start.32 = (f32[1536]{0:T(1024)S(1)}, f32[1536]{0:T(1024)}, u32[]{:S(2)}) copy-start(f32[1536]{0:T(1024)} %param.31) | copy-start | bytes 18436
  190.5 149.9 %all-gather.5.cloned.1.call-start = ((), (), s32[]{:S(2)}) async-start(), calls=%async_computation.6 | async-start | bytes 2506752 | tf_op jit(solution)/shard_map/all_gather | solution.py:64
  192.2 1.7 collective-permute-start
  196.1 9.8 collective-permute-start.1
  208.2 15.3 %collective-permute-start.2 = (bf16[192,1536]{1,0:T(8,128)(2,1)}, bf16[192,1536]{1,0:T(8,128)(2,1)}, u32[]{:S(2)}, u32[]{:S(2)}) collective-permute-start(bf16[192,1536]{1,0:T(8,128)(2,1)} %maximum_select_fusion.2), channel_id=1, source_target_pairs={{0,8},{2,10},{4,12},{6,14},{8,0},{10,2},{12,4},{14,6},{16,24},{18,... | collective-permute-start | bytes 1769480 | tf_op jit(solution)/shard_map/ppermute | solution.py:16
  209.8 252.8 %all-reduce.21.cloned.1.call-start = ((), (), s32[]{:S(2)}) async-start(), calls=%async_computation.7 | async-start | bytes 6881280 | tf_op jit(solution)/shard_map/psum | solution.py:148
  226.4 61.2 %collective-permute-start.3 = (bf16[384,1536]{1,0:T(8,128)(2,1)}, bf16[384,1536]{1,0:T(8,128)(2,1)}, u32[]{:S(2)}, u32[]{:S(2)}) collective-permute-start(bf16[384,1536]{1,0:T(8,128)(2,1)} %maximum_select_fusion.1), channel_id=1, source_target_pairs={{0,16},{2,18},{4,20},{6,22},{8,24},{10,26},{12,28},{14,30},{16,0},... | collective-permute-start | bytes 3538952 | tf_op jit(solution)/shard_map/ppermute | solution.py:16
  281.6 3.3 copy-start.1
  287.6 18.2 %copy-start.18 = (f32[8,280]{1,0:T(8,128)}, f32[8,280]{1,0:T(8,128)S(1)}, u32[]{:S(2)}) copy-start(f32[8,280]{1,0:T(8,128)S(1)} %fusion.111) | copy-start | bytes 26884
  287.6 18.2 %copy-start.25 = (f32[1536]{0:T(1024)S(1)}, f32[1536]{0:T(1024)}, u32[]{:S(2)}) copy-start(f32[1536]{0:T(1024)} %convert_convert_fusion) | copy-start | bytes 18436
  370.2 364.1 %all-reduce.23.cloned.1.call-start = ((), (), s32[]{:S(2)}) async-start(), calls=%async_computation.12 | async-start | bytes 13762560 | tf_op jit(solution)/shard_map/psum | solution.py:131
  462.7 6.4 copy-start.14
  462.7 6.4 copy-start.2
  462.7 6.4 copy-start.5
  462.7 6.4 copy-start.19
  462.7 6.4 copy-start.23
  469.0 5.6 copy-start.7
  469.0 5.6 copy-start.16
  474.7 7.6 copy-start.8
  553.3 7.2 copy-start.39
  557.5 2.9 copy-start.6
  568.2 7.9 copy-start.20
  568.2 7.9 copy-start.24
  568.2 7.9 copy-start.35
  568.2 253.0 %reduce-scatter.7.cloned.1.call-start = ((), (), s32[]{:S(2)}) async-start(), calls=%async_computation.9 | async-start | bytes 1253376 | tf_op jit(solution)/shard_map/reduce_scatter | solution.py:214
  576.0 12.8 %copy-start.17 = (f32[8,280]{1,0:T(8,128)S(1)}, f32[8,280]{1,0:T(8,128)}, u32[]{:S(2)}) copy-start(f32[8,280]{1,0:T(8,128)} %fusion.109) | copy-start | bytes 26884
  576.0 299.7 %reduce-scatter.9.cloned.1.call-start = ((), (), s32[]{:S(2)}) async-start(), calls=%async_computation.10 | async-start | bytes 5013504 | tf_op jit(solution)/shard_map/reduce_scatter | solution.py:215
  588.7 11.4 %copy-start.10 = (f32[8,280]{1,0:T(8,128)S(1)}, f32[8,280]{1,0:T(8,128)}, u32[]{:S(2)}) copy-start(f32[8,280]{1,0:T(8,128)} %copy-done.9) | copy-start | bytes 26884
  588.7 11.4 %copy-start.15 = (f32[8,280]{1,0:T(8,128)S(1)}, f32[8,280]{1,0:T(8,128)}, u32[]{:S(2)}) copy-start(f32[8,280]{1,0:T(8,128)} %fusion.110) | copy-start | bytes 26884
  588.7 11.4 %copy-start.22 = (f32[768]{0:T(1024)S(1)}, f32[768]{0:T(1024)}, u32[]{:S(2)}) copy-start(f32[768]{0:T(1024)} %copy-done.21) | copy-start | bytes 9220
  588.7 11.4 %copy-start.34 = (f32[768]{0:T(1024)S(1)}, f32[768]{0:T(1024)}, u32[]{:S(2)}) copy-start(f32[768]{0:T(1024)} %convert_element_type.174) | copy-start | bytes 9220
  588.7 366.2 %reduce-scatter.11.cloned.1.call-start = ((), (), s32[]{:S(2)}) async-start(), calls=%async_computation.11 | async-start | bytes 5013504 | tf_op jit(solution)/shard_map/reduce_scatter | solution.py:216
  599.8 14.0 %copy-start.36 = (bf16[768]{0:T(1024)(128)(2,1)S(1)}, bf16[768]{0:T(1024)(128)(2,1)}, u32[]{:S(2)}) copy-start(bf16[768]{0:T(1024)(128)(2,1)} %get-tuple-element.167) | copy-start | bytes 4612
  599.8 426.9 %reduce-scatter.5.cloned.1.call-start = ((), (), s32[]{:S(2)}) async-start(), calls=%async_computation.8 | async-start | bytes 3760128 | tf_op jit(solution)/shard_map/reduce_scatter | solution.py:213
  614.5 124.0 %copy-start.12 = (f32[8,280]{1,0:T(8,128)S(1)}, f32[8,280]{1,0:T(8,128)}, u32[]{:S(2)}) copy-start(f32[8,280]{1,0:T(8,128)} %copy-done.11) | copy-start | bytes 26884
  734.3 4.2 copy-start.4
  734.3 8.5 copy-start.26
  734.3 8.5 copy-start.27
  734.3 8.5 copy-start.30
  734.3 8.5 copy-start.31
  (5 other events, 6.2 us)
Sparse Core Ops, SparseCore 0:
  10.9 43.1 all-gather.2
  190.6 90.9 all-reduce.18
  284.4 42.3 all-gather.4
  370.4 92.2 all-reduce.20
  568.3 165.9 all-reduce.22
  738.4 58.2 reduce-scatter.6
  801.0 74.6 reduce-scatter.8
  880.1 74.7 reduce-scatter.10
  959.4 67.3 reduce-scatter.4
